TPU v7x, 512 devices: a whole 4x8x8 slice. The times are simulated.
512 devices in a mesh: section: 16 (over x_lo, z), latent: 32 (over x_hi, y, core).
Axes of the slice: x: 4 (x_hi: 2, x_lo: 2; x = x_hi * 2 + x_lo), y: 8, z: 8, core: 2. Of those that a mesh axis runs over, the one named last changes fastest.
Arguments:
- residual: bfloat16 [4, 320, 4608], P(None, None, 'latent'), may hold values from -6 to 6
- encoder: bfloat16 [16, 4608, 4096], P('section', None, 'latent'), may hold values from -0.09375 to 0.09375
- enc_bias: float32 [16, 4096], P('section', 'latent'), may hold values from -4 to 4
- gate_code: int32 [16, 4096], P('section', 'latent'), may hold values from 0 to 2
- decoder: bfloat16 [16, 3, 4096, 4608], P('section', None, 'latent'), may hold values from -0.0546875 to 0.0546875
Outputs:
- reconstruction: bfloat16 [16, 80, 4608], P('section', None, 'latent')
- latent_acts: bfloat16 [16, 320, 4096], P('section', None, 'latent')
Inputs may be any that keep to these rules, and one draw needn't show every extreme that they name: `gate_code`: 0: the latent is always active; 1: its threshold is zero; 2: it is never active.
All inputs are finite; a program needn't handle non-finite values.
Results may differ from a plain program's by a relative error of at most 0.019.
Values may be sent and summed in bfloat16 or wider, within the bound.
A program may use at most 64 MiB of HBM per device.

v0:
```python
import jax
import jax.numpy as jnp
from jax import lax
from jax.sharding import PartitionSpec as P

LAYERS = 4


def swapped(shard, axis, stride):
    return lax.ppermute(shard, axis, [(i, i ^ 1 << stride) for i in range(lax.axis_size(axis))])


def passed_along(value, axis, steps):
    count = lax.axis_size(axis)
    first, last = (max(0, -steps), min(count, count - steps))
    return lax.ppermute(value, axis, [(source, source + steps) for source in range(first, last)])


def group_reduce(partial_rows, group_size):
    current = partial_rows
    section_index = lax.axis_index("section")
    level_count = group_size.bit_length() - 1
    for level in reversed(range(level_count)):
        half = current.shape[0] // 2
        lower = current[:half]
        upper = current[half:]
        high_side = section_index // 2**level % 2 == 1
        kept = jnp.where(high_side, upper, lower)
        sent = jnp.where(high_side, lower, upper)
        received = swapped(sent.astype(jnp.bfloat16), "section", level).astype(sent.dtype)
        current = kept + received
    return current


def shards(residual, encoder, enc_bias, gate_code, decoder):
    group_size = lax.axis_size("section") // LAYERS
    layer_index = lax.axis_index("section") // group_size
    resid_layer = lax.dynamic_index_in_dim(residual, layer_index, 0, keepdims=False)
    enc_local = encoder[0]
    preact = jnp.dot(
        lax.all_gather(resid_layer, "latent", axis=1, tiled=True),
        enc_local,
        preferred_element_type=jnp.float32,
    )
    preact = preact + enc_bias[0]
    threshold = 10000.0 * (gate_code[0].astype(jnp.float32) - 1.0)
    active_vals = jnp.where(preact > threshold, preact, jnp.zeros_like(preact)).astype(jnp.bfloat16)
    reach_count = decoder.shape[1]
    sources = [active_vals]
    carried = active_vals
    for hop_index in range(1, reach_count):
        carried = passed_along(carried, "section", group_size)
        sources.append(carried)
    stacked = jnp.stack(sources, axis=0)
    dec_local = decoder[0]
    own_share = lax.psum_scatter(
        lax.dot_general(
            dec_local, stacked, (((0, 1), (0, 2)), ((), ())), preferred_element_type=jnp.float32
        ).astype(jnp.bfloat16),
        "latent",
        scatter_dimension=0,
        tiled=True,
    ).astype(jnp.float32)
    summed = jnp.transpose(own_share)
    rebuilt = group_reduce(summed, group_size).astype(jnp.bfloat16)
    return (rebuilt[None], active_vals[None])


def solution(mesh):
    return jax.shard_map(
        shards,
        mesh=mesh,
        in_specs=(
            P(None, None, "latent"),
            P("section", None, "latent"),
            P("section", "latent"),
            P("section", "latent"),
            P("section", None, "latent", None),
        ),
        out_specs=(P("section", None, "latent"), P("section", None, "latent")),
        check_vma=False,
    )
```

profile of v0, /device:TPU:16, one launch (start us, length us, event | category | flops | bytes accessed | tf_op | source)
XLA Modules:
  0.0 296.9 jit_solution(9694946097347359255)
XLA Ops:
  7.2 0.0 copy-start
  7.2 0.0 all-gather.3.cloned.1.call-start
  7.2 1.7 constant_dynamic-slice_fusion
  8.9 0.0 all-gather.3.cloned.1.call-update
  9.0 0.0 reduce-scatter.4.cloned.1.call-start
  9.0 0.7 multiply_bitcast_fusion
  9.7 94.1 %all-gather.3.cloned.1.call-done = bf16[1,320,4608]{1,2,0:T(8,128)(2,1)} async-done(((bf16[1,320,144]{1,2,0:T(8,128)(2,1)}), bf16[1,320,4608]{1,2,0:T(8,128)(2,1)}) %all-gather.3.cloned.1.call-update) | async-done | bytes 2949136 | tf_op jit(solution)/shard_map/all_gather | solution.py:41
  103.8 3.5 %fusion.15 = bf16[320,128]{1,0:T(8,128)(2,1)S(1)} fusion(bf16[1,4608,128]{2,1,0:T(8,128)(2,1)} %param.6, bf16[1,320,4608]{1,2,0:T(8,128)(2,1)} %all-gather.3.cloned.1.call-done, f32[128]{0:T(128)S(1)} %multiply_bitcast_fusion, f32[128]{0:T(128)} %bitcast.44), kind=kOutput, calls=%fused_computation.9 | convolution fusion | flops 377651200 | bytes 4211712 | tf_op jit(solution)/shard_map/dot_general | solution.py:40
  107.3 0.0 copy-start.2
  107.3 8.0 %collective-permute-start = (bf16[320,128]{1,0:T(8,128)(2,1)S(1)}, bf16[320,128]{1,0:T(8,128)(2,1)S(1)}, u32[]{:S(2)}, u32[]{:S(2)}) collective-permute-start(bf16[320,128]{1,0:T(8,128)(2,1)S(1)} %fusion.15), channel_id=1, source_target_pairs={{0,128},{32,160},{64,192},{96,224},{128,256},{160,288},{192,320},{... | collective-permute-start | bytes 245768 | tf_op jit(solution)/shard_map/ppermute | solution.py:16
  115.3 2.1 collective-permute-done
  117.5 9.9 %collective-permute-start.1 = (bf16[320,128]{1,0:T(8,128)(2,1)S(1)}, bf16[320,128]{1,0:T(8,128)(2,1)S(1)}, u32[]{:S(2)}, u32[]{:S(2)}) collective-permute-start(bf16[320,128]{1,0:T(8,128)(2,1)S(1)} %collective-permute-done), channel_id=1, source_target_pairs={{0,128},{32,160},{64,192},{96,224},{128,256},{160,288},{192,320},{... | collective-permute-start | bytes 245768 | tf_op jit(solution)/shard_map/ppermute | solution.py:16
  127.3 3.7 %collective-permute-done.1 = bf16[320,128]{1,0:T(8,128)(2,1)S(1)} collective-permute-done((bf16[320,128]{1,0:T(8,128)(2,1)S(1)}, bf16[320,128]{1,0:T(8,128)(2,1)S(1)}, u32[]{:S(2)}, u32[]{:S(2)}) %collective-permute-start.1) | collective-permute-done | bytes 81952 | tf_op jit(solution)/shard_map/ppermute | solution.py:16
  131.0 0.0 copy-done.2
  131.0 0.0 copy-done
  131.0 3.3 %fusion.1 = bf16[4608,320]{0,1:T(8,128)(2,1)} fusion(bf16[1,3,128,4608]{3,2,1,0:T(8,128)(2,1)S(1)} %copy-done, bf16[1,320,128]{2,1,0:T(8,128)(2,1)S(1)} %bitcast.43, bf16[1,320,128]{2,1,0:T(8,128)(2,1)S(1)} %bitcast.42, bf16[1,320,128]{2,1,0:T(8,128)(2,1)S(1)} %bitcast.40), kind=kOutput, calls=%fused_computation.2 | convolution fusion | flops 1134182400 | bytes 6733824 | tf_op jit(solution)/shard_map/dot_general | solution.py:57
  134.3 5.5 %copy.9 = bf16[4608,320]{1,0:T(8,128)(2,1)} copy(bf16[4608,320]{0,1:T(8,128)(2,1)} %fusion.1) | data formatting | bytes 5898240
  139.8 0.0 reduce-scatter.4.cloned.1.call-update
  139.9 129.5 %reduce-scatter.4.cloned.1.call-done = bf16[144,320]{1,0:T(8,128)(2,1)} async-done(((bf16[4608,320]{1,0:T(8,128)(2,1)}), bf16[144,320]{1,0:T(8,128)(2,1)}) %reduce-scatter.4.cloned.1.call-update) | async-done | bytes 92176
  269.4 1.7 copy.10
  271.0 0.9 convert_bitcast_fusion
  272.0 0.0 copy-start.1
  272.0 0.7 copy-done.1
  272.7 0.7 select_convert_fusion
  273.4 4.6 %collective-permute-start.2 = (bf16[160,144]{1,0:T(8,128)(2,1)}, bf16[160,144]{1,0:T(8,128)(2,1)}, u32[]{:S(2)}, u32[]{:S(2)}) collective-permute-start(bf16[160,144]{1,0:T(8,128)(2,1)} %select_convert_fusion), channel_id=1, source_target_pairs={{0,64},{32,96},{64,0},{96,32},{128,192},{160,224},{192,128},{224,1... | collective-permute-start | bytes 138248 | tf_op jit(solution)/shard_map/ppermute | solution.py:10
  278.0 2.9 collective-permute-done.2
  280.9 1.1 convert_add_fusion
  282.0 3.6 %collective-permute-start.3 = (bf16[80,144]{1,0:T(8,128)(2,1)S(1)}, bf16[80,144]{1,0:T(8,128)(2,1)S(1)}, u32[]{:S(2)}, u32[]{:S(2)}) collective-permute-start(bf16[80,144]{1,0:T(8,128)(2,1)S(1)} %select_convert_fusion.1), channel_id=1, source_target_pairs={{0,32},{32,0},{64,96},{96,64},{128,160},{160,128},{192,224},{224,1... | collective-permute-start | bytes 69128 | tf_op jit(solution)/shard_map/ppermute | solution.py:10
  285.6 2.3 collective-permute-done.3
  287.9 0.6 fusion.25
  288.5 1.5 copy.8
  (1 shorter events, 0.0 us)
Async XLA Ops:
  7.2 123.9 %copy-start = (bf16[1,3,128,4608]{3,2,1,0:T(8,128)(2,1)S(1)}, bf16[1,3,128,4608]{3,2,1,0:T(8,128)(2,1)}, u32[]{:S(2)}) copy-start(bf16[1,3,128,4608]{3,2,1,0:T(8,128)(2,1)} %param.9) | copy-start | bytes 10616836
  7.2 96.6 %all-gather.3.cloned.1.call-start = ((), (), s32[]{:S(2)}) async-start(), calls=%async_computation.1 | async-start | bytes 3649536 | tf_op jit(solution)/shard_map/all_gather | solution.py:41
  9.0 260.4 %reduce-scatter.4.cloned.1.call-start = ((), (), s32[]{:S(2)}) async-start(), calls=%async_computation.2 | async-start | bytes 3649536
  107.3 23.7 %copy-start.2 = (bf16[320,128]{1,0:T(8,128)(2,1)}, bf16[320,128]{1,0:T(8,128)(2,1)S(1)}, u32[]{:S(2)}) copy-start(bf16[320,128]{1,0:T(8,128)(2,1)S(1)} %fusion.15) | copy-start | bytes 245764
  107.3 10.2 %collective-permute-start = (bf16[320,128]{1,0:T(8,128)(2,1)S(1)}, bf16[320,128]{1,0:T(8,128)(2,1)S(1)}, u32[]{:S(2)}, u32[]{:S(2)}) collective-permute-start(bf16[320,128]{1,0:T(8,128)(2,1)S(1)} %fusion.15), channel_id=1, source_target_pairs={{0,128},{32,160},{64,192},{96,224},{128,256},{160,288},{192,320},{... | collective-permute-start | bytes 245768 | tf_op jit(solution)/shard_map/ppermute | solution.py:16
  117.5 13.6 %collective-permute-start.1 = (bf16[320,128]{1,0:T(8,128)(2,1)S(1)}, bf16[320,128]{1,0:T(8,128)(2,1)S(1)}, u32[]{:S(2)}, u32[]{:S(2)}) collective-permute-start(bf16[320,128]{1,0:T(8,128)(2,1)S(1)} %collective-permute-done), channel_id=1, source_target_pairs={{0,128},{32,160},{64,192},{96,224},{128,256},{160,288},{192,320},{... | collective-permute-start | bytes 245768 | tf_op jit(solution)/shard_map/ppermute | solution.py:16
  272.0 0.7 copy-start.1
  273.4 7.5 %collective-permute-start.2 = (bf16[160,144]{1,0:T(8,128)(2,1)}, bf16[160,144]{1,0:T(8,128)(2,1)}, u32[]{:S(2)}, u32[]{:S(2)}) collective-permute-start(bf16[160,144]{1,0:T(8,128)(2,1)} %select_convert_fusion), channel_id=1, source_target_pairs={{0,64},{32,96},{64,0},{96,32},{128,192},{160,224},{192,128},{224,1... | collective-permute-start | bytes 138248 | tf_op jit(solution)/shard_map/ppermute | solution.py:10
  282.0 5.9 %collective-permute-start.3 = (bf16[80,144]{1,0:T(8,128)(2,1)S(1)}, bf16[80,144]{1,0:T(8,128)(2,1)S(1)}, u32[]{:S(2)}, u32[]{:S(2)}) collective-permute-start(bf16[80,144]{1,0:T(8,128)(2,1)S(1)} %select_convert_fusion.1), channel_id=1, source_target_pairs={{0,32},{32,0},{64,96},{96,64},{128,160},{160,128},{192,224},{224,1... | collective-permute-start | bytes 69128 | tf_op jit(solution)/shard_map/ppermute | solution.py:10
Sparse Core Ops, SparseCore 0:
  11.3 92.4 all-gather.2
  140.0 129.3 reduce-scatter.3
where the time goes:
time: 297 us
  waiting for transfers between devices  235 us (79%)
  starting transfers between devices  26.2 us (9%)
  between operations  14.2 us (5%)
  local copies, waits for them, and re-layouts  11.1 us (4%)
  matrix products  6.78 us (2%)
  other arithmetic  3.95 us (1%)
    unnamed x3, waiting for transfers between devices  130 us
    all_gather x1, waiting for transfers between devices, shards(): lax.all_gather(resid_layer, 'latent', axis=1, tiled=True)  94.1 us
    ppermute x2, starting transfers between devices, passed_along(): lax.ppermute(value, axis, [(source, source + steps) for source in range(f...  17.9 us
    unnamed x9, local copies, waits for them, and re-layouts  9.42 us
    ppermute x2, starting transfers between devices, swapped(): lax.ppermute(shard, axis, [(i, i ^ 1 << stride) for i in range(lax.axis_s...  8.22 us
  transfers between devices with their start and end apart: 6, of which 6 were waited for; matrix products, arithmetic and copies ran while one was open for 0% of the time, Pallas kernels for 0%

commit v1 on v0

--- a/solution.py
+++ b/solution.py
@@ -38,7 +38,10 @@
     resid_layer = lax.dynamic_index_in_dim(residual, layer_index, 0, keepdims=False)
     enc_local = encoder[0]
     preact = jnp.dot(
-        lax.all_gather(resid_layer, "latent", axis=1, tiled=True),
+        jnp.concatenate(
+            lax.all_to_all(jnp.stack([resid_layer] * lax.axis_size("latent")), "latent", 0, 0),
+            axis=1,
+        ),
         enc_local,
         preferred_element_type=jnp.float32,
     )

time: 297 us -> 298 us (level)
  waiting for transfers between devices: 235 us -> 223 us
  starting transfers between devices: 26.2 us -> 38 us
    all_gather x1 -> x0, waiting for transfers between devices: 94.1 us -> none  [shards(): lax.all_gather(resid_layer, 'latent', axis=1, tiled=True)]
    all_to_all x0 -> x1, waiting for transfers between devices: none -> 78.1 us  [shards(): lax.all_to_all(jnp.stack([resid_layer] * lax.axis_size('latent')), 'laten...]
    all_to_all x0 -> x1, starting transfers between devices: none -> 10.2 us  [shards(): lax.all_to_all(jnp.stack([resid_layer] * lax.axis_size('latent')), 'laten...]
    unnamed x3 -> x2, waiting for transfers between devices: 130 us -> 133 us
    unnamed x9 -> x13, local copies, waits for them, and re-layouts: 9.42 us -> 9.43 us
where the time goes in v1:
time: 298 us
  waiting for transfers between devices  223 us (75%)
  starting transfers between devices  38 us (13%)
  between operations  14.2 us (5%)
  local copies, waits for them, and re-layouts  12.6 us (4%)
  matrix products  6.75 us (2%)
  other arithmetic  3.29 us (1%)
    unnamed x2, waiting for transfers between devices  133 us
    all_to_all x1, waiting for transfers between devices, shards(): lax.all_to_all(jnp.stack([resid_layer] * lax.axis_size('latent')), 'laten...  78.1 us
    ppermute x2, starting transfers between devices, passed_along(): lax.ppermute(value, axis, [(source, source + steps) for source in range(f...  19.5 us
    all_to_all x1, starting transfers between devices, shards(): lax.all_to_all(jnp.stack([resid_layer] * lax.axis_size('latent')), 'laten...  10.2 us
    unnamed x13, local copies, waits for them, and re-layouts  9.43 us
    ppermute x2, starting transfers between devices, swapped(): lax.ppermute(shard, axis, [(i, i ^ 1 << stride) for i in range(lax.axis_s...  8.29 us
    ppermute x2, waiting for transfers between devices, passed_along(): lax.ppermute(value, axis, [(source, source + steps) for source in range(f...  7.24 us
  transfers between devices with their start and end apart: 6, of which 6 were waited for; matrix products, arithmetic and copies ran while one was open for 0% of the time, Pallas kernels for 0%

profile of v1, /device:TPU:16, one launch (start us, length us, event | category | flops | bytes accessed | tf_op | source)
XLA Modules:
  0.0 297.9 jit_solution(5947142344105284638)
XLA Ops:
  7.2 0.0 copy-start
  7.2 1.1 dynamic-slice_bitcast_fusion
  8.3 2.1 stack.10
  10.4 0.0 copy-start.4
  10.4 0.0 copy-start.3
  10.4 10.2 %all-to-all-start = ((bf16[32,320,144]{1,2,0:T(8,128)(2,1)}), bf16[32,320,144]{1,2,0:T(8,128)(2,1)}, u32[]{:S(2)}, u32[]{:S(2)}) async-start(bf16[32,320,144]{1,2,0:T(8,128)(2,1)} %stack.10), calls=%async_computation | async-start | bytes 7077888 | tf_op jit(solution)/shard_map/all_to_all | solution.py:42
  20.6 0.0 reduce-scatter.4.cloned.1.call-start
  20.7 0.0 copy-done.4
  20.7 78.1 %all-to-all-done = bf16[32,320,144]{1,2,0:T(8,128)(2,1)} async-done(((bf16[32,320,144]{1,2,0:T(8,128)(2,1)}), bf16[32,320,144]{1,2,0:T(8,128)(2,1)}, u32[]{:S(2)}, u32[]{:S(2)}) %all-to-all-start) | async-done | bytes 2949152 | tf_op jit(solution)/shard_map/all_to_all | solution.py:42
  98.8 0.0 copy-done.3
  98.8 3.5 %fusion.10 = bf16[320,128]{1,0:T(8,128)(2,1)S(1)} fusion(bf16[320,4608]{0,1:T(8,128)(2,1)} %bitcast.2, bf16[1,4608,128]{2,1,0:T(8,128)(2,1)} %param.6, f32[128]{0:T(128)S(1)} %multiply_bitcast_fusion, f32[128]{0:T(128)S(1)} %bitcast.41), kind=kOutput, calls=%fused_computation.8 | convolution fusion | flops 377651200 | bytes 4211712 | tf_op jit(solution)/shard_map/dot_general | solution.py:40
  102.2 0.0 copy-start.2
  102.2 11.2 %collective-permute-start = (bf16[320,128]{1,0:T(8,128)(2,1)S(1)}, bf16[320,128]{1,0:T(8,128)(2,1)S(1)}, u32[]{:S(2)}, u32[]{:S(2)}) collective-permute-start(bf16[320,128]{1,0:T(8,128)(2,1)S(1)} %fusion.10), channel_id=1, source_target_pairs={{0,128},{32,160},{64,192},{96,224},{128,256},{160,288},{192,320},{... | collective-permute-start | bytes 245768 | tf_op jit(solution)/shard_map/ppermute | solution.py:16
  113.5 3.6 %collective-permute-done = bf16[320,128]{1,0:T(8,128)(2,1)S(1)} collective-permute-done((bf16[320,128]{1,0:T(8,128)(2,1)S(1)}, bf16[320,128]{1,0:T(8,128)(2,1)S(1)}, u32[]{:S(2)}, u32[]{:S(2)}) %collective-permute-start) | collective-permute-done | bytes 81952 | tf_op jit(solution)/shard_map/ppermute | solution.py:16
  117.1 8.3 %collective-permute-start.1 = (bf16[320,128]{1,0:T(8,128)(2,1)S(1)}, bf16[320,128]{1,0:T(8,128)(2,1)S(1)}, u32[]{:S(2)}, u32[]{:S(2)}) collective-permute-start(bf16[320,128]{1,0:T(8,128)(2,1)S(1)} %collective-permute-done), channel_id=1, source_target_pairs={{0,128},{32,160},{64,192},{96,224},{128,256},{160,288},{192,320},{... | collective-permute-start | bytes 245768 | tf_op jit(solution)/shard_map/ppermute | solution.py:16
  125.3 3.6 %collective-permute-done.1 = bf16[320,128]{1,0:T(8,128)(2,1)S(1)} collective-permute-done((bf16[320,128]{1,0:T(8,128)(2,1)S(1)}, bf16[320,128]{1,0:T(8,128)(2,1)S(1)}, u32[]{:S(2)}, u32[]{:S(2)}) %collective-permute-start.1) | collective-permute-done | bytes 81952 | tf_op jit(solution)/shard_map/ppermute | solution.py:16
  129.0 0.0 copy-done.2
  129.0 0.0 copy-done
  129.0 3.3 %fusion.1 = bf16[4608,320]{0,1:T(8,128)(2,1)} fusion(bf16[1,3,128,4608]{3,2,1,0:T(8,128)(2,1)S(1)} %copy-done, bf16[1,320,128]{2,1,0:T(8,128)(2,1)S(1)} %bitcast.40, bf16[1,320,128]{2,1,0:T(8,128)(2,1)S(1)} %bitcast.39, bf16[1,320,128]{2,1,0:T(8,128)(2,1)S(1)} %bitcast.37), kind=kOutput, calls=%fused_computation.2 | convolution fusion | flops 1134182400 | bytes 6733824 | tf_op jit(solution)/shard_map/dot_general | solution.py:60
  132.3 5.5 %copy.10 = bf16[4608,320]{1,0:T(8,128)(2,1)} copy(bf16[4608,320]{0,1:T(8,128)(2,1)} %fusion.1) | data formatting | bytes 5898240
  137.8 0.0 reduce-scatter.4.cloned.1.call-update
  137.8 132.6 %reduce-scatter.4.cloned.1.call-done = bf16[144,320]{1,0:T(8,128)(2,1)} async-done(((bf16[4608,320]{1,0:T(8,128)(2,1)}), bf16[144,320]{1,0:T(8,128)(2,1)}) %reduce-scatter.4.cloned.1.call-update) | async-done | bytes 92176
  270.4 1.7 copy.11
  272.1 0.9 convert_bitcast_fusion
  273.0 0.0 copy-start.1
  273.0 0.7 copy-done.1
  273.7 0.7 select_convert_fusion
  274.4 4.7 %collective-permute-start.2 = (bf16[160,144]{1,0:T(8,128)(2,1)}, bf16[160,144]{1,0:T(8,128)(2,1)}, u32[]{:S(2)}, u32[]{:S(2)}) collective-permute-start(bf16[160,144]{1,0:T(8,128)(2,1)} %select_convert_fusion), channel_id=1, source_target_pairs={{0,64},{32,96},{64,0},{96,32},{128,192},{160,224},{192,128},{224,1... | collective-permute-start | bytes 138248 | tf_op jit(solution)/shard_map/ppermute | solution.py:10
  279.1 2.9 collective-permute-done.2
  282.0 1.1 convert_add_fusion
  283.0 3.6 %collective-permute-start.3 = (bf16[80,144]{1,0:T(8,128)(2,1)S(1)}, bf16[80,144]{1,0:T(8,128)(2,1)S(1)}, u32[]{:S(2)}, u32[]{:S(2)}) collective-permute-start(bf16[80,144]{1,0:T(8,128)(2,1)S(1)} %select_convert_fusion.1), channel_id=1, source_target_pairs={{0,32},{32,0},{64,96},{96,64},{128,160},{160,128},{192,224},{224,1... | collective-permute-start | bytes 69128 | tf_op jit(solution)/shard_map/ppermute | solution.py:10
  286.7 2.3 collective-permute-done.3
  288.9 0.6 fusion.18
  289.6 1.5 copy.9
  (2 shorter events, 0.0 us)
Async XLA Ops:
  7.2 121.8 %copy-start = (bf16[1,3,128,4608]{3,2,1,0:T(8,128)(2,1)S(1)}, bf16[1,3,128,4608]{3,2,1,0:T(8,128)(2,1)}, u32[]{:S(2)}) copy-start(bf16[1,3,128,4608]{3,2,1,0:T(8,128)(2,1)} %param.9) | copy-start | bytes 10616836
  10.4 10.3 %copy-start.4 = (s32[1,128]{1,0:T(1,128)S(1)}, s32[1,128]{1,0:T(1,128)}, u32[]{:S(2)}) copy-start(s32[1,128]{1,0:T(1,128)} %param.8) | copy-start | bytes 1540
  10.4 88.4 %copy-start.3 = (f32[1,128]{1,0:T(1,128)S(1)}, f32[1,128]{1,0:T(1,128)}, u32[]{:S(2)}) copy-start(f32[1,128]{1,0:T(1,128)} %param.7) | copy-start | bytes 1540
  10.4 88.4 %all-to-all-start = ((bf16[32,320,144]{1,2,0:T(8,128)(2,1)}), bf16[32,320,144]{1,2,0:T(8,128)(2,1)}, u32[]{:S(2)}, u32[]{:S(2)}) async-start(bf16[32,320,144]{1,2,0:T(8,128)(2,1)} %stack.10), calls=%async_computation | async-start | bytes 7077888 | tf_op jit(solution)/shard_map/all_to_all | solution.py:42
  20.6 249.8 %reduce-scatter.4.cloned.1.call-start = ((), (), s32[]{:S(2)}) async-start(), calls=%async_computation.2 | async-start | bytes 3649536
  102.2 26.7 %copy-start.2 = (bf16[320,128]{1,0:T(8,128)(2,1)}, bf16[320,128]{1,0:T(8,128)(2,1)S(1)}, u32[]{:S(2)}) copy-start(bf16[320,128]{1,0:T(8,128)(2,1)S(1)} %fusion.10) | copy-start | bytes 245764
  102.2 14.8 %collective-permute-start = (bf16[320,128]{1,0:T(8,128)(2,1)S(1)}, bf16[320,128]{1,0:T(8,128)(2,1)S(1)}, u32[]{:S(2)}, u32[]{:S(2)}) collective-permute-start(bf16[320,128]{1,0:T(8,128)(2,1)S(1)} %fusion.10), channel_id=1, source_target_pairs={{0,128},{32,160},{64,192},{96,224},{128,256},{160,288},{192,320},{... | collective-permute-start | bytes 245768 | tf_op jit(solution)/shard_map/ppermute | solution.py:16
  117.1 11.9 %collective-permute-start.1 = (bf16[320,128]{1,0:T(8,128)(2,1)S(1)}, bf16[320,128]{1,0:T(8,128)(2,1)S(1)}, u32[]{:S(2)}, u32[]{:S(2)}) collective-permute-start(bf16[320,128]{1,0:T(8,128)(2,1)S(1)} %collective-permute-done), channel_id=1, source_target_pairs={{0,128},{32,160},{64,192},{96,224},{128,256},{160,288},{192,320},{... | collective-permute-start | bytes 245768 | tf_op jit(solution)/shard_map/ppermute | solution.py:16
  273.0 0.7 copy-start.1
  274.4 7.6 %collective-permute-start.2 = (bf16[160,144]{1,0:T(8,128)(2,1)}, bf16[160,144]{1,0:T(8,128)(2,1)}, u32[]{:S(2)}, u32[]{:S(2)}) collective-permute-start(bf16[160,144]{1,0:T(8,128)(2,1)} %select_convert_fusion), channel_id=1, source_target_pairs={{0,64},{32,96},{64,0},{96,32},{128,192},{160,224},{192,128},{224,1... | collective-permute-start | bytes 138248 | tf_op jit(solution)/shard_map/ppermute | solution.py:10
  283.0 5.9 %collective-permute-start.3 = (bf16[80,144]{1,0:T(8,128)(2,1)S(1)}, bf16[80,144]{1,0:T(8,128)(2,1)S(1)}, u32[]{:S(2)}, u32[]{:S(2)}) collective-permute-start(bf16[80,144]{1,0:T(8,128)(2,1)S(1)} %select_convert_fusion.1), channel_id=1, source_target_pairs={{0,32},{32,0},{64,96},{96,64},{128,160},{160,128},{192,224},{224,1... | collective-permute-start | bytes 69128 | tf_op jit(solution)/shard_map/ppermute | solution.py:10
Sparse Core Ops, SparseCore 0:
  137.9 132.4 reduce-scatter.3
